TPU v7x, 32 devices: a whole 2x2x4 slice. The times are simulated.
32 devices in a mesh: row: 16 (over z, x, core), col: 2 (over y).
Axes of the slice: x: 2, y: 2, z: 4, core: 2. Of those that a mesh axis runs over, the one named last changes fastest.
Arguments:
- counts: int32 [8192, 32768], P('row', 'col'), may hold values from 0 to 63
- row_support: int32 [8192], P(('row', 'col')), may hold values from 1 to 2209
- col_support: int32 [32768], P(('col', 'row')), may hold values from 1 to 2209
- total: int32 [1], replicated, may hold values from 256 to 4095
- sketch: bfloat16 [32768, 256], P('col'), may hold values from -6 to 6
Outputs:
- left_basis: float32 [8192, 256], P('row')
- right_basis: float32 [32768, 256], P('col')
All inputs are finite; a program needn't handle non-finite values.
Results may differ from a plain program's by a relative error of at most 0.012.
Values may be sent and summed in bfloat16 or wider, within the bound.
A program may use at most 192 MiB of HBM per device.

v0:
```python
import jax
import jax.numpy as jnp
from jax import lax
from jax.sharding import PartitionSpec as P


def lift(block, row_part, col_part, total):
    value = jnp.log(jnp.maximum(block, 1).astype(jnp.float32))
    value = value + jnp.log(total[0].astype(jnp.float32))
    value = value - jnp.log(row_part.astype(jnp.float32))[:, None]
    value = value - jnp.log(col_part.astype(jnp.float32))[None, :]
    return jnp.where(block > 0, jnp.maximum(value, 0.0), 0.0).astype(jnp.bfloat16)


def factor_of(gram):
    return jnp.linalg.cholesky(gram)


def solve_rows(lower, matrix):
    return jax.scipy.linalg.solve_triangular(lower, matrix.T, lower=True).T


def gram_of(matrix):
    return jnp.dot(matrix.T, matrix, precision=lax.Precision.HIGHEST)


def per_device(counts, row_support, col_support, total, sketch):
    row_local = lax.all_gather(row_support, "col", axis=0, tiled=True)
    col_local = lax.all_gather(col_support, "row", axis=0, tiled=True)
    table = lift(counts, row_local, col_local, total)
    row_count = table.shape[0]
    col_count = table.shape[1]

    def left_orth(rhs, narrow):
        whole = lax.psum(jnp.dot(table, rhs, preferred_element_type=jnp.float32), "col")
        gram = lax.psum(gram_of(whole), "row")
        basis = solve_rows(factor_of(gram), whole)
        if narrow:
            return basis.astype(jnp.bfloat16)
        return basis

    q_first = left_orth(sketch, True)
    partial_value = lax.dot_general(
        table, q_first, (((0,), (0,)), ((), ())), preferred_element_type=jnp.float32
    )
    whole = lax.psum(partial_value, "row")
    gram = lax.psum(gram_of(whole), "col")
    q_second = solve_rows(factor_of(gram), whole)
    q_third = left_orth(q_second.astype(jnp.bfloat16), False)
    total_rows = row_count * lax.axis_size("row")
    total_cols = col_count * lax.axis_size("col")
    return (
        q_third * jnp.sqrt(jnp.float32(total_rows)),
        q_second * jnp.sqrt(jnp.float32(total_cols)),
    )


def solution(mesh):
    in_specs = (P("row", "col"), P(("row", "col")), P(("col", "row")), P(), P("col", None))
    out_specs = (P("row", None), P("col", None))
    return jax.shard_map(
        per_device, mesh=mesh, in_specs=in_specs, out_specs=out_specs, check_vma=False
    )
```

profile of v0, /device:TPU:0, one launch (start us, length us, event | category | flops | bytes accessed | tf_op | source)
XLA Modules:
  0.0 932.7 jit_solution(9221446948077840741)
XLA Ops:
  7.2 23.5 %all_gather.7 = s32[16384]{0:T(1024)S(1)} all-gather(s32[1024]{0:T(1024)} %param.10), channel_id=1, replica_groups=mesh['row'=16,'col'=2] {'row'}, dimensions={0}, use_global_device_ids=true | all-gather | bytes 69632 | tf_op jit(solution)/shard_map/all_gather | solution.py:29
  30.7 4.5 all-gather
  35.9 17.1 %select_convert_fusion = bf16[512,16384]{1,0:T(8,128)(2,1)S(1)} fusion(s32[512,16384]{1,0:T(8,128)} %param.8, f32[16384]{0:T(1024)S(1)} %convert_log_fusion, f32[512]{0:T(512)S(1)} %bitcast.119, f32[]{:T(128)} %bitcast), kind=kLoop, calls=%fused_computation.6 | loop fusion | flops 75497472 | bytes 50399236 | tf_op jit(solution)/shard_map/convert_element_type | solution.py:12
  53.0 6.2 copy-done.2
  59.2 7.7 fusion.42
  67.0 26.0 %all-reduce.8.cloned.1.call-done = f32[512,256]{1,0:T(8,128)} async-done(((f32[512,256]{1,0:T(8,128)}), f32[512,256]{1,0:T(8,128)}) %all-reduce.8.cloned.1.call-update) | async-done | bytes 524304 | tf_op jit(solution)/shard_map/psum | solution.py:35
  96.2 90.5 %all-reduce.10.cloned.1.call-done = f32[256,256]{0,1:T(8,128)} async-done(((f32[256,256]{0,1:T(8,128)}), f32[256,256]{0,1:T(8,128)}) %all-reduce.10.cloned.1.call-update) | async-done | bytes 262160 | tf_op jit(solution)/shard_map/psum | solution.py:36
  188.8 11.7 %cholesky.172 = f32[128,128]{1,0:T(8,128)S(1)} custom-call(f32[128,128]{1,0:T(8,128)S(1)} %cholesky.270), custom_call_target="Cholesky" | custom-call | tf_op jit(solution)/shard_map/jit(cholesky)/cholesky | solution.py:16
  200.6 9.8 %custom-call.19 = f32[1,128,128]{1,2,0:T(8,128)S(1)} custom-call(f32[1,128,128]{2,1,0:T(8,128)S(1)} %get-tuple-element.73), custom_call_target="InvertDiagBlocksLowerTriangular" | custom-call | tf_op jit(solution)/shard_map/jit(cholesky)/cholesky | solution.py:16
  210.9 11.7 %cholesky.189 = f32[128,128]{1,0:T(8,128)S(1)} custom-call(f32[128,128]{1,0:T(8,128)S(1)} %convolution_subtract_fusion.5), custom_call_target="Cholesky" | custom-call | tf_op jit(solution)/shard_map/jit(cholesky)/cholesky | solution.py:16
  224.9 4.5 while.6
  229.4 19.7 %custom-call.20 = f32[2,128,128]{1,2,0:T(8,128)S(1)} custom-call(f32[2,128,128]{2,1,0:T(8,128)S(1)} %get-tuple-element.26), custom_call_target="InvertDiagBlocksLowerTriangular" | custom-call | tf_op jit(solution)/shard_map/jit(_solve_triangular)/triangular_solve | solution.py:20
  252.4 16.1 %fusion.6 = f32[16384,256]{1,0:T(8,128)} fusion(bf16[512,16384]{1,0:T(8,128)(2,1)} %copy-done.2, bf16[128,512]{1,0:T(8,128)(2,1)S(1)} %fusion.23, f32[128,512]{1,0:T(8,128)S(1)} %fusion.9), kind=kOutput, calls=%fused_computation.25 | convolution fusion | flops 4295491584 | bytes 33947648 | tf_op jit(solution)/shard_map/dot_general | solution.py:43
  268.6 298.5 %all-reduce.12.cloned.1.call-done = f32[16384,256]{1,0:T(8,128)} async-done(((f32[16384,256]{1,0:T(8,128)}), f32[16384,256]{1,0:T(8,128)}) %all-reduce.12.cloned.1.call-update) | async-done | bytes 16777232 | tf_op jit(solution)/shard_map/psum | solution.py:46
  567.1 37.8 %fusion.44 = f32[256,256]{0,1:T(8,128)} fusion(f32[16384,256]{1,0:T(8,128)} %all-reduce.12.cloned.1.call-done), kind=kOutput, calls=%fused_computation.95 | convolution fusion | flops 12884901888 | bytes 17039360 | tf_op jit(solution)/shard_map/dot_general | solution.py:24
  605.0 23.0 %all-reduce.14.cloned.1.call-done = f32[256,256]{0,1:T(8,128)} async-done(((f32[256,256]{0,1:T(8,128)}), f32[256,256]{0,1:T(8,128)}) %all-reduce.14.cloned.1.call-update) | async-done | bytes 262160 | tf_op jit(solution)/shard_map/psum | solution.py:47
  630.1 11.7 %cholesky.206 = f32[128,128]{1,0:T(8,128)S(1)} custom-call(f32[128,128]{1,0:T(8,128)S(1)} %cholesky.273), custom_call_target="Cholesky" | custom-call | tf_op jit(solution)/shard_map/jit(cholesky)/cholesky | solution.py:16
  641.9 9.8 %custom-call.21 = f32[1,128,128]{1,2,0:T(8,128)S(1)} custom-call(f32[1,128,128]{2,1,0:T(8,128)S(1)} %get-tuple-element.69), custom_call_target="InvertDiagBlocksLowerTriangular" | custom-call | tf_op jit(solution)/shard_map/jit(cholesky)/cholesky | solution.py:16
  652.2 11.7 %cholesky.223 = f32[128,128]{1,0:T(8,128)S(1)} custom-call(f32[128,128]{1,0:T(8,128)S(1)} %convolution_subtract_fusion.4), custom_call_target="Cholesky" | custom-call | tf_op jit(solution)/shard_map/jit(cholesky)/cholesky | solution.py:16
  670.3 19.7 %custom-call.15 = f32[2,128,128]{1,2,0:T(8,128)S(1)} custom-call(f32[2,128,128]{2,1,0:T(8,128)S(1)} %get-tuple-element.19), custom_call_target="InvertDiagBlocksLowerTriangular" | custom-call | tf_op jit(solution)/shard_map/jit(_solve_triangular)/triangular_solve | solution.py:20
  690.0 10.8 %fusion.3 = f32[128,16384]{1,0:T(8,128)S(1)} fusion(f32[256,16384]{0,1:T(8,128)} %bitcast.113, f32[2,128,128]{1,2,0:T(8,128)S(1)} %custom-call.15), kind=kOutput, calls=%fused_computation.12 | convolution fusion | flops 3221225472 | bytes 16842752 | tf_op jit(solution)/shard_map/jit(_solve_triangular)/triangular_solve | solution.py:20
  700.8 13.4 %convolution_subtract_fusion = f32[128,16384]{0,1:T(8,128)S(1)} fusion(f32[128,16384]{1,0:T(8,128)S(1)} %fusion.3, f32[256,16384]{0,1:T(8,128)S(1)} %bitcast.114, f32[256,256]{1,0:T(8,128)S(1)} %get-tuple-element.225), kind=kOutput, calls=%fused_computation.7 | convolution fusion | flops 3223322624 | bytes 25231360 | tf_op jit(solution)/shard_map/jit(_solve_triangular)/triangular_solve | solution.py:20
  714.2 9.8 %fusion.19 = f32[128,16384]{1,0:T(8,128)} fusion(f32[128,16384]{0,1:T(8,128)S(1)} %convolution_subtract_fusion, f32[2,128,128]{1,2,0:T(8,128)S(1)} %custom-call.15), kind=kOutput, calls=%fused_computation.45 | convolution fusion | flops 3221225472 | bytes 16842752 | tf_op jit(solution)/shard_map/jit(_solve_triangular)/triangular_solve | solution.py:20
  724.0 13.7 %fusion.1 = f32[512,256]{1,0:T(8,128)} fusion(bf16[512,16384]{1,0:T(8,128)(2,1)} %copy-done.2, f32[128,16384]{1,0:T(8,128)} %fusion.19, f32[128,16384]{1,0:T(8,128)} %copy-done.1), kind=kOutput, calls=%fused_computation.11 | convolution fusion | flops 4311744512 | bytes 34078720 | tf_op jit(solution)/shard_map/dot_general | solution.py:35
  737.8 28.8 %all-reduce.16.cloned.1.call-done = f32[512,256]{1,0:T(8,128)} async-done(((f32[512,256]{1,0:T(8,128)}), f32[512,256]{1,0:T(8,128)}) %all-reduce.16.cloned.1.call-update) | async-done | bytes 524304 | tf_op jit(solution)/shard_map/psum | solution.py:35
  769.5 12.1 %multiply_bitcast_fusion = f32[16384,256]{0,1:T(8,128)} fusion(f32[128,16384]{1,0:T(8,128)} %fusion.19, f32[128,16384]{1,0:T(8,128)} %copy-done.1), kind=kLoop, calls=%fused_computation.9 | loop fusion | flops 8388608 | bytes 33554432 | tf_op jit(solution)/shard_map/mul | solution.py:54
  781.6 17.5 %copy.22 = f32[16384,256]{1,0:T(8,128)} copy(f32[16384,256]{0,1:T(8,128)} %multiply_bitcast_fusion) | data formatting | bytes 33554432
  799.2 61.0 %all-reduce.18.cloned.1.call-done = f32[256,256]{0,1:T(8,128)} async-done(((f32[256,256]{0,1:T(8,128)}), f32[256,256]{0,1:T(8,128)}) %all-reduce.18.cloned.1.call-update) | async-done | bytes 262160 | tf_op jit(solution)/shard_map/psum | solution.py:36
  862.2 11.7 %cholesky.240 = f32[128,128]{1,0:T(8,128)S(1)} custom-call(f32[128,128]{1,0:T(8,128)S(1)} %cholesky.276), custom_call_target="Cholesky" | custom-call | tf_op jit(solution)/shard_map/jit(cholesky)/cholesky | solution.py:16
  874.0 9.8 %custom-call.22 = f32[1,128,128]{1,2,0:T(8,128)S(1)} custom-call(f32[1,128,128]{2,1,0:T(8,128)S(1)} %get-tuple-element.65), custom_call_target="InvertDiagBlocksLowerTriangular" | custom-call | tf_op jit(solution)/shard_map/jit(cholesky)/cholesky | solution.py:16
  884.3 11.7 %cholesky.257 = f32[128,128]{1,0:T(8,128)S(1)} custom-call(f32[128,128]{1,0:T(8,128)S(1)} %convolution_subtract_fusion.3), custom_call_target="Cholesky" | custom-call | tf_op jit(solution)/shard_map/jit(cholesky)/cholesky | solution.py:16
  902.9 20.0 %custom-call.23 = f32[2,128,128]{1,2,0:T(8,128)S(1)} custom-call(f32[2,128,128]{2,1,0:T(8,128)S(1)} %get-tuple-element.27), custom_call_target="InvertDiagBlocksLowerTriangular" | custom-call | tf_op jit(solution)/shard_map/jit(_solve_triangular)/triangular_solve | solution.py:20
  (88 shorter events, 43.5 us)
Async XLA Ops:
  7.2 85.9 %all-reduce.8.cloned.1.call-start = ((), (), s32[]{:S(2)}) async-start(), calls=%async_computation | async-start | bytes 1048576 | tf_op jit(solution)/shard_map/psum | solution.py:35
  53.0 6.2 copy-start.2
  67.0 119.8 %all-reduce.10.cloned.1.call-start = ((), (), s32[]{:S(2)}) async-start(), calls=%async_computation.1 | async-start | bytes 524288 | tf_op jit(solution)/shard_map/psum | solution.py:36
  96.0 471.1 %all-reduce.12.cloned.1.call-start = ((), (), s32[]{:S(2)}) async-start(), calls=%async_computation.2 | async-start | bytes 33554432 | tf_op jit(solution)/shard_map/psum | solution.py:46
  268.5 359.5 %all-reduce.14.cloned.1.call-start = ((), (), s32[]{:S(2)}) async-start(), calls=%async_computation.3 | async-start | bytes 524288 | tf_op jit(solution)/shard_map/psum | solution.py:47
  605.0 161.6 %all-reduce.16.cloned.1.call-start = ((), (), s32[]{:S(2)}) async-start(), calls=%async_computation.4 | async-start | bytes 1048576 | tf_op jit(solution)/shard_map/psum | solution.py:35
  690.0 10.8 %copy-start = (f32[16384,256]{1,0:T(8,128)S(1)}, f32[16384,256]{1,0:T(8,128)}, u32[]{:S(2)}) copy-start(f32[16384,256]{1,0:T(8,128)} %all-reduce.12.cloned.1.call-done) | copy-start | bytes 50331652
  700.8 13.4 %copy-start.1 = (f32[128,16384]{1,0:T(8,128)}, f32[128,16384]{1,0:T(8,128)S(1)}, u32[]{:S(2)}) copy-start(f32[128,16384]{1,0:T(8,128)S(1)} %fusion.3) | copy-start | bytes 25165828
  737.7 122.4 %all-reduce.18.cloned.1.call-start = ((), (), s32[]{:S(2)}) async-start(), calls=%async_computation.5 | async-start | bytes 524288 | tf_op jit(solution)/shard_map/psum | solution.py:36
  781.6 141.2 %copy-start.3 = (f32[512,256]{1,0:T(8,128)S(1)}, f32[512,256]{1,0:T(8,128)}, u32[]{:S(2)}) copy-start(f32[512,256]{1,0:T(8,128)} %all-reduce.16.cloned.1.call-done) | copy-start | bytes 1572868
Sparse Core Ops, SparseCore 0:
  67.1 25.9 all-reduce.7
  97.0 89.7 all-reduce.9
  268.7 298.4 all-reduce.11
  605.1 22.9 all-reduce.13
  737.9 28.6 all-reduce.15
  770.4 89.6 all-reduce.17
where the time goes:
time: 938 us; the launch traced here: 933 us
  waiting for transfers between devices  528 us (56%)
  other arithmetic  195 us (21%)
  matrix products  121 us (13%)
  local copies, waits for them, and re-layouts  40 us (4%)
  blocking collectives  28 us (3%)
  between operations  19.6 us (2%)
    psum x1, waiting for transfers between devices, per_device(): whole = lax.psum(partial_value, 'row')  299 us
    psum x2, waiting for transfers between devices, left_orth(): gram = lax.psum(gram_of(whole), 'row')  151 us
    another operation x20, other arithmetic, factor_of(): return jnp.linalg.cholesky(gram)  103 us
    another operation x7, other arithmetic, solve_rows(): return jax.scipy.linalg.solve_triangular(lower, matrix.T, lower=True).T  59.4 us
    psum x2, waiting for transfers between devices, left_orth(): lax.psum(jnp.dot(table, rhs, preferred_element_type=jnp.float32), 'col')  54.8 us
    dot_general x3, matrix products, gram_of(): return jnp.dot(matrix.T, matrix, precision=lax.Precision.HIGHEST)  43.6 us
    another operation x9, matrix products, solve_rows(): return jax.scipy.linalg.solve_triangular(lower, matrix.T, lower=True).T  38.7 us
    unnamed x10, local copies, waits for them, and re-layouts  24.7 us
  transfers between devices with their start and end apart: 6, of which 6 were waited for; matrix products, arithmetic and copies ran while one was open for 3% of the time, Pallas kernels for 0%

commit v1 on v0

--- a/solution.py
+++ b/solution.py
@@ -33,7 +33,7 @@
 
     def left_orth(rhs, narrow):
         whole = lax.psum(jnp.dot(table, rhs, preferred_element_type=jnp.float32), "col")
-        gram = lax.psum(gram_of(whole), "row")
+        gram = jnp.sum(lax.all_gather(gram_of(whole), "row"), axis=0)
         basis = solve_rows(factor_of(gram), whole)
         if narrow:
             return basis.astype(jnp.bfloat16)

time: 938 us -> 857 us (0.914)
  waiting for transfers between devices: 528 us -> 445 us
    psum x2 -> x0, waiting for transfers between devices: 151 us -> none  [left_orth(): gram = lax.psum(gram_of(whole), 'row')]
    all_gather x0 -> x2, waiting for transfers between devices: none -> 70.8 us  [left_orth(): gram = jnp.sum(lax.all_gather(gram_of(whole), 'row'), axis=0)]
  transfers between devices with their start and end apart: 6 -> 6, of which waited for: 6 -> 6; matrix products, arithmetic and copies ran while one was open for 3% -> 4% of each run, Pallas kernels for 0% -> 0%
where the time goes in v1:
time: 857 us; the launch traced here: 851 us
  waiting for transfers between devices  445 us (52%)
  other arithmetic  198 us (23%)
  matrix products  121 us (14%)
  local copies, waits for them, and re-layouts  38.1 us (4%)
  blocking collectives  28 us (3%)
  between operations  19.3 us (2%)
    psum x1, waiting for transfers between devices, per_device(): whole = lax.psum(partial_value, 'row')  297 us
    another operation x20, other arithmetic, factor_of(): return jnp.linalg.cholesky(gram)  103 us
    all_gather x2, waiting for transfers between devices, left_orth(): gram = jnp.sum(lax.all_gather(gram_of(whole), 'row'), axis=0)  70.8 us
    another operation x7, other arithmetic, solve_rows(): return jax.scipy.linalg.solve_triangular(lower, matrix.T, lower=True).T  59.3 us
    psum x2, waiting for transfers between devices, left_orth(): lax.psum(jnp.dot(table, rhs, preferred_element_type=jnp.float32), 'col')  54.8 us
    dot_general x3, matrix products, gram_of(): return jnp.dot(matrix.T, matrix, precision=lax.Precision.HIGHEST)  43.7 us
    another operation x9, matrix products, solve_rows(): return jax.scipy.linalg.solve_triangular(lower, matrix.T, lower=True).T  38.7 us
    unnamed x10, local copies, waits for them, and re-layouts  24.7 us
  transfers between devices with their start and end apart: 6, of which 6 were waited for; matrix products, arithmetic and copies ran while one was open for 4% of the time, Pallas kernels for 0%

profile of v1, /device:TPU:0, one launch (start us, length us, event | category | flops | bytes accessed | tf_op | source)
XLA Modules:
  0.0 851.4 jit_solution(6707301712329133888)
XLA Ops:
  7.2 23.5 %all_gather.19 = s32[16384]{0:T(1024)S(1)} all-gather(s32[1024]{0:T(1024)} %param.10), channel_id=1, replica_groups=mesh['row'=16,'col'=2] {'row'}, dimensions={0}, use_global_device_ids=true | all-gather | bytes 69632 | tf_op jit(solution)/shard_map/all_gather | solution.py:29
  30.7 4.5 all-gather.2
  35.9 17.1 %select_convert_fusion = bf16[512,16384]{1,0:T(8,128)(2,1)S(1)} fusion(s32[512,16384]{1,0:T(8,128)} %param.8, f32[16384]{0:T(1024)S(1)} %convert_log_fusion, f32[512]{0:T(512)S(1)} %bitcast.123, f32[]{:T(128)} %bitcast), kind=kLoop, calls=%fused_computation.6 | loop fusion | flops 75497472 | bytes 50399236 | tf_op jit(solution)/shard_map/convert_element_type | solution.py:12
  53.0 6.2 copy-done.2
  59.2 7.8 fusion.42
  67.0 26.0 %all-reduce.6.cloned.1.call-done = f32[512,256]{1,0:T(8,128)} async-done(((f32[512,256]{1,0:T(8,128)}), f32[512,256]{1,0:T(8,128)}) %all-reduce.6.cloned.1.call-update) | async-done | bytes 524304 | tf_op jit(solution)/shard_map/psum | solution.py:35
  96.3 50.2 %all-gather.6.cloned.1.call-done = f32[4096,256]{1,0:T(8,128)} async-done(((f32[256,256]{1,0:T(8,128)}), f32[4096,256]{1,0:T(8,128)}) %all-gather.6.cloned.1.call-update) | async-done | bytes 4194320 | tf_op jit(solution)/shard_map/all_gather | solution.py:36
  149.2 11.7 %cholesky.172 = f32[128,128]{1,0:T(8,128)S(1)} custom-call(f32[128,128]{1,0:T(8,128)S(1)} %cholesky.270), custom_call_target="Cholesky" | custom-call | tf_op jit(solution)/shard_map/jit(cholesky)/cholesky | solution.py:16
  161.0 9.8 %custom-call.19 = f32[1,128,128]{1,2,0:T(8,128)S(1)} custom-call(f32[1,128,128]{2,1,0:T(8,128)S(1)} %get-tuple-element.73), custom_call_target="InvertDiagBlocksLowerTriangular" | custom-call | tf_op jit(solution)/shard_map/jit(cholesky)/cholesky | solution.py:16
  171.2 11.7 %cholesky.189 = f32[128,128]{1,0:T(8,128)S(1)} custom-call(f32[128,128]{1,0:T(8,128)S(1)} %convolution_subtract_fusion.5), custom_call_target="Cholesky" | custom-call | tf_op jit(solution)/shard_map/jit(cholesky)/cholesky | solution.py:16
  185.2 4.6 while.6
  189.8 19.7 %custom-call.20 = f32[2,128,128]{1,2,0:T(8,128)S(1)} custom-call(f32[2,128,128]{2,1,0:T(8,128)S(1)} %get-tuple-element.26), custom_call_target="InvertDiagBlocksLowerTriangular" | custom-call | tf_op jit(solution)/shard_map/jit(_solve_triangular)/triangular_solve | solution.py:20
  212.9 16.1 %fusion.6 = f32[16384,256]{1,0:T(8,128)} fusion(bf16[512,16384]{1,0:T(8,128)(2,1)} %copy-done.2, bf16[128,512]{1,0:T(8,128)(2,1)S(1)} %fusion.23, f32[128,512]{1,0:T(8,128)S(1)} %fusion.9), kind=kOutput, calls=%fused_computation.25 | convolution fusion | flops 4295491584 | bytes 33947648 | tf_op jit(solution)/shard_map/dot_general | solution.py:43
  229.0 296.6 %all-reduce.8.cloned.1.call-done = f32[16384,256]{1,0:T(8,128)} async-done(((f32[16384,256]{1,0:T(8,128)}), f32[16384,256]{1,0:T(8,128)}) %all-reduce.8.cloned.1.call-update) | async-done | bytes 16777232 | tf_op jit(solution)/shard_map/psum | solution.py:46
  525.6 37.8 %fusion.44 = f32[256,256]{0,1:T(8,128)} fusion(f32[16384,256]{1,0:T(8,128)} %all-reduce.8.cloned.1.call-done), kind=kOutput, calls=%fused_computation.95 | convolution fusion | flops 12884901888 | bytes 17039360 | tf_op jit(solution)/shard_map/dot_general | solution.py:24
  563.5 23.0 %all-reduce.10.cloned.1.call-done = f32[256,256]{0,1:T(8,128)} async-done(((f32[256,256]{0,1:T(8,128)}), f32[256,256]{0,1:T(8,128)}) %all-reduce.10.cloned.1.call-update) | async-done | bytes 262160 | tf_op jit(solution)/shard_map/psum | solution.py:47
  588.6 11.7 %cholesky.206 = f32[128,128]{1,0:T(8,128)S(1)} custom-call(f32[128,128]{1,0:T(8,128)S(1)} %cholesky.273), custom_call_target="Cholesky" | custom-call | tf_op jit(solution)/shard_map/jit(cholesky)/cholesky | solution.py:16
  600.4 9.8 %custom-call.21 = f32[1,128,128]{1,2,0:T(8,128)S(1)} custom-call(f32[1,128,128]{2,1,0:T(8,128)S(1)} %get-tuple-element.69), custom_call_target="InvertDiagBlocksLowerTriangular" | custom-call | tf_op jit(solution)/shard_map/jit(cholesky)/cholesky | solution.py:16
  610.7 11.7 %cholesky.223 = f32[128,128]{1,0:T(8,128)S(1)} custom-call(f32[128,128]{1,0:T(8,128)S(1)} %convolution_subtract_fusion.4), custom_call_target="Cholesky" | custom-call | tf_op jit(solution)/shard_map/jit(cholesky)/cholesky | solution.py:16
  628.8 19.7 %custom-call.15 = f32[2,128,128]{1,2,0:T(8,128)S(1)} custom-call(f32[2,128,128]{2,1,0:T(8,128)S(1)} %get-tuple-element.19), custom_call_target="InvertDiagBlocksLowerTriangular" | custom-call | tf_op jit(solution)/shard_map/jit(_solve_triangular)/triangular_solve | solution.py:20
  648.5 10.8 %fusion.3 = f32[128,16384]{1,0:T(8,128)S(1)} fusion(f32[256,16384]{0,1:T(8,128)} %bitcast.115, f32[2,128,128]{1,2,0:T(8,128)S(1)} %custom-call.15), kind=kOutput, calls=%fused_computation.12 | convolution fusion | flops 3221225472 | bytes 16842752 | tf_op jit(solution)/shard_map/jit(_solve_triangular)/triangular_solve | solution.py:20
  659.3 13.4 %convolution_subtract_fusion = f32[128,16384]{0,1:T(8,128)S(1)} fusion(f32[128,16384]{1,0:T(8,128)S(1)} %fusion.3, f32[256,16384]{0,1:T(8,128)S(1)} %bitcast.116, f32[256,256]{1,0:T(8,128)S(1)} %get-tuple-element.227), kind=kOutput, calls=%fused_computation.7 | convolution fusion | flops 3223322624 | bytes 25231360 | tf_op jit(solution)/shard_map/jit(_solve_triangular)/triangular_solve | solution.py:20
  672.7 9.8 %fusion.19 = f32[128,16384]{1,0:T(8,128)} fusion(f32[128,16384]{0,1:T(8,128)S(1)} %convolution_subtract_fusion, f32[2,128,128]{1,2,0:T(8,128)S(1)} %custom-call.15), kind=kOutput, calls=%fused_computation.45 | convolution fusion | flops 3221225472 | bytes 16842752 | tf_op jit(solution)/shard_map/jit(_solve_triangular)/triangular_solve | solution.py:20
  682.5 13.7 %fusion.1 = f32[512,256]{1,0:T(8,128)} fusion(bf16[512,16384]{1,0:T(8,128)(2,1)} %copy-done.2, f32[128,16384]{1,0:T(8,128)} %fusion.19, f32[128,16384]{1,0:T(8,128)} %copy-done.1), kind=kOutput, calls=%fused_computation.11 | convolution fusion | flops 4311744512 | bytes 34078720 | tf_op jit(solution)/shard_map/dot_general | solution.py:35
  696.3 28.8 %all-reduce.12.cloned.1.call-done = f32[512,256]{1,0:T(8,128)} async-done(((f32[512,256]{1,0:T(8,128)}), f32[512,256]{1,0:T(8,128)}) %all-reduce.12.cloned.1.call-update) | async-done | bytes 524304 | tf_op jit(solution)/shard_map/psum | solution.py:35
  728.1 12.4 %multiply_bitcast_fusion = f32[16384,256]{0,1:T(8,128)} fusion(f32[128,16384]{1,0:T(8,128)} %fusion.19, f32[128,16384]{1,0:T(8,128)} %copy-done.1), kind=kLoop, calls=%fused_computation.9 | loop fusion | flops 8388608 | bytes 33554432 | tf_op jit(solution)/shard_map/mul | solution.py:54
  740.5 17.6 %copy.18 = f32[16384,256]{1,0:T(8,128)} copy(f32[16384,256]{0,1:T(8,128)} %multiply_bitcast_fusion) | data formatting | bytes 33554432
  758.0 20.6 %all-gather.8.cloned.1.call-done = f32[4096,256]{1,0:T(8,128)} async-done(((f32[256,256]{1,0:T(8,128)}), f32[4096,256]{1,0:T(8,128)}) %all-gather.8.cloned.1.call-update) | async-done | bytes 4194320 | tf_op jit(solution)/shard_map/all_gather | solution.py:36
  781.3 11.7 %cholesky.240 = f32[128,128]{1,0:T(8,128)S(1)} custom-call(f32[128,128]{1,0:T(8,128)S(1)} %cholesky.276), custom_call_target="Cholesky" | custom-call | tf_op jit(solution)/shard_map/jit(cholesky)/cholesky | solution.py:16
  793.1 9.8 %custom-call.22 = f32[1,128,128]{1,2,0:T(8,128)S(1)} custom-call(f32[1,128,128]{2,1,0:T(8,128)S(1)} %get-tuple-element.65), custom_call_target="InvertDiagBlocksLowerTriangular" | custom-call | tf_op jit(solution)/shard_map/jit(cholesky)/cholesky | solution.py:16
  803.4 11.7 %cholesky.257 = f32[128,128]{1,0:T(8,128)S(1)} custom-call(f32[128,128]{1,0:T(8,128)S(1)} %convolution_subtract_fusion.3), custom_call_target="Cholesky" | custom-call | tf_op jit(solution)/shard_map/jit(cholesky)/cholesky | solution.py:16
  822.0 19.8 %custom-call.23 = f32[2,128,128]{1,2,0:T(8,128)S(1)} custom-call(f32[2,128,128]{2,1,0:T(8,128)S(1)} %get-tuple-element.27), custom_call_target="InvertDiagBlocksLowerTriangular" | custom-call | tf_op jit(solution)/shard_map/jit(_solve_triangular)/triangular_solve | solution.py:20
  (90 shorter events, 44.8 us)
Async XLA Ops:
  7.2 85.9 %all-reduce.6.cloned.1.call-start = ((), (), s32[]{:S(2)}) async-start(), calls=%async_computation | async-start | bytes 1048576 | tf_op jit(solution)/shard_map/psum | solution.py:35
  53.0 6.2 copy-start.2
  67.0 79.5 %all-gather.6.cloned.1.call-start = ((), (), s32[]{:S(2)}) async-start(), calls=%async_computation.4 | async-start | bytes 4456448 | tf_op jit(solution)/shard_map/all_gather | solution.py:36
  96.0 429.6 %all-reduce.8.cloned.1.call-start = ((), (), s32[]{:S(2)}) async-start(), calls=%async_computation.1 | async-start | bytes 33554432 | tf_op jit(solution)/shard_map/psum | solution.py:46
  229.0 357.6 %all-reduce.10.cloned.1.call-start = ((), (), s32[]{:S(2)}) async-start(), calls=%async_computation.2 | async-start | bytes 524288 | tf_op jit(solution)/shard_map/psum | solution.py:47
  563.5 161.6 %all-reduce.12.cloned.1.call-start = ((), (), s32[]{:S(2)}) async-start(), calls=%async_computation.3 | async-start | bytes 1048576 | tf_op jit(solution)/shard_map/psum | solution.py:35
  648.5 10.8 %copy-start = (f32[16384,256]{1,0:T(8,128)S(1)}, f32[16384,256]{1,0:T(8,128)}, u32[]{:S(2)}) copy-start(f32[16384,256]{1,0:T(8,128)} %all-reduce.8.cloned.1.call-done) | copy-start | bytes 50331652
  659.3 13.4 %copy-start.1 = (f32[128,16384]{1,0:T(8,128)}, f32[128,16384]{1,0:T(8,128)S(1)}, u32[]{:S(2)}) copy-start(f32[128,16384]{1,0:T(8,128)S(1)} %fusion.3) | copy-start | bytes 25165828
  696.3 82.4 %all-gather.8.cloned.1.call-start = ((), (), s32[]{:S(2)}) async-start(), calls=%async_computation.5 | async-start | bytes 4456448 | tf_op jit(solution)/shard_map/all_gather | solution.py:36
  740.5 101.4 %copy-start.3 = (f32[512,256]{1,0:T(8,128)S(1)}, f32[512,256]{1,0:T(8,128)}, u32[]{:S(2)}) copy-start(f32[512,256]{1,0:T(8,128)} %all-reduce.12.cloned.1.call-done) | copy-start | bytes 1572868
Sparse Core Ops, SparseCore 0:
  67.1 25.9 all-reduce.5
  96.1 50.3 all-gather.5
  229.1 296.4 all-reduce.7
  563.6 22.9 all-reduce.9
  696.4 28.6 all-reduce.11
  728.2 50.3 all-gather.7
